TPU v7x, 256 devices: a whole 4x4x8 slice. The times are simulated.
256 devices in a mesh: member: 2 (over core), rep: 8 (over z), tensor: 16 (over x, y).
Axes of the slice: x: 4, y: 4, z: 8, core: 2. Of those that a mesh axis runs over, the one named last changes fastest.
Arguments:
- queries: bfloat16 [2, 64, 32, 128], P('member', 'rep'), parts along dimension 1, may hold values from -110 to 110
- keys: bfloat16 [2, 64, 8192, 128], P('member', 'rep', 'tensor'), parts along dimension 1, may hold values from -4.2 to 4.2
- values: bfloat16 [2, 64, 8192, 128], P('member', 'rep', 'tensor'), parts along dimension 1, may hold values from -6 to 6
- lengths: int32 [64], P('rep'), parts along dimension 0, may hold values from 256 to 2048, as said below
- targets: int32 [64], P('rep'), parts along dimension 0, may hold values from 0 to 16383
- residual: bfloat16 [2, 64, 4096], P('member', 'rep'), parts along dimension 1, may hold values from -32 to 32
- out_weight: bfloat16 [2, 4096, 4096], P('member', 'tensor'), may hold values from -0.75 to 0.75
- norm_gain: float32 [2, 4096], P('member'), may hold values from 0.5 to 1.5
- head_weight: bfloat16 [2, 4096, 16384], P('member', None, 'tensor'), may hold values from -0.2 to 0.2878906
Outputs:
- mean_logprobs: float32 [64, 16384], P(('rep', 'member'), 'tensor'), parts along dimension 0
- target_logprob: float32 [64], P(('rep', 'member')), parts along dimension 0
There are 8 independent parts, one for each index of `rep`. A program takes and returns all parts, laid end to end along the dimension named above; an argument that names none is the same for every part. Nothing has to cross between parts.
Inputs may be any that keep to these rules, and one draw needn't show every extreme that they name: `lengths`: some row of every draw has all 2048 slots live.
All inputs are finite; a program needn't handle non-finite values.
Results may differ from a plain program's by a relative error of at most 0.004.
Values may be sent and summed in bfloat16 or wider, within the bound.
A program may use at most 64 MiB of HBM per device.

v0:
```python
import jax
import jax.numpy as jnp
from jax import lax
from jax.sharding import PartitionSpec as P

HEADS = 32
KV_HEADS = 4


def for_sending(shard):

    def short(part):
        return part.astype(jnp.bfloat16) if part.dtype == jnp.float32 else part

    return jax.tree.map(short, shard)


def swapped(block, axis, distance):
    count = lax.axis_size(axis)
    route = []
    for low in range(count):
        high = low | 1 << distance
        if high != low and high < count:
            route += [(low, high), (high, low)]
    return lax.ppermute(block, axis, route)


def join_partial(earlier, later):
    peak_one, total_one, weighted_one = earlier
    peak_two, total_two, weighted_two = later
    peak_new = jnp.maximum(peak_one, peak_two)
    scale_one = jnp.exp(peak_one - peak_new)
    scale_two = jnp.exp(peak_two - peak_new)
    total_new = total_one * scale_one + total_two * scale_two
    weighted_new = weighted_one * scale_one[..., None] + weighted_two * scale_two[..., None]
    return (peak_new, total_new, weighted_new)


def local(queries, keys, values, lengths, targets, residual, out_weight, norm_gain, head_weight):
    axis_width = lax.axis_size("tensor")
    my_rank = lax.axis_index("tensor")
    member_rank = lax.axis_index("member")
    group_size = axis_width // KV_HEADS
    heads_kv = HEADS // KV_HEADS
    heads_dev = HEADS // axis_width
    row_count = keys.shape[1]
    key_span = keys.shape[2]
    head_depth = keys.shape[3]
    kv_index = my_rank // group_size
    slot_first = my_rank % group_size * key_span
    group_query = lax.dynamic_slice_in_dim(queries[0], kv_index * heads_kv, heads_kv, 1)
    scores = jnp.einsum("rqd,rcd->rqc", group_query, keys[0], preferred_element_type=jnp.float32)
    scores = scores * (1.0 / head_depth**0.5)
    slot_ids = slot_first + jnp.arange(key_span, dtype=jnp.int32)
    live = (slot_ids[None, :] < lengths[:, None])[:, None, :]
    scores = jnp.where(live, scores, jnp.float32(-1e30))
    top_score = jnp.max(scores, axis=-1)
    weights = jnp.where(live, jnp.exp(scores - top_score[..., None]), jnp.float32(0.0))
    weight_total = jnp.sum(weights, axis=-1)
    weighted = jnp.einsum(
        "rqc,rcd->rqd", weights.astype(jnp.bfloat16), values[0], preferred_element_type=jnp.float32
    )
    state = (top_score, weight_total, weighted)
    for level in range(group_size.bit_length() - 1):
        partner = swapped(
            (for_sending(state[0]), for_sending(state[1]), for_sending(state[2])), "tensor", level
        )
        state = join_partial(state, partner)
    top_score, weight_total, weighted = state
    head_first = my_rank % group_size * heads_dev
    own_total = lax.dynamic_slice_in_dim(weight_total, head_first, heads_dev, 1)
    own_weighted = lax.dynamic_slice_in_dim(weighted, head_first, heads_dev, 1)
    attended = (
        (own_weighted / own_total[..., None])
        .reshape(row_count, heads_dev * head_depth)
        .astype(jnp.bfloat16)
    )
    projected = jnp.dot(attended, out_weight[0], preferred_element_type=jnp.float32)
    stream = residual[0].astype(jnp.float32)
    summed = lax.psum(projected.astype(jnp.bfloat16), "tensor").astype(jnp.float32)
    hidden = stream + summed
    scaled = (
        hidden * lax.rsqrt(jnp.mean(hidden * hidden, axis=-1, keepdims=True) + 1e-05) * norm_gain[0]
    )
    normed = scaled.astype(jnp.bfloat16)
    logits = jnp.dot(normed, head_weight[0], preferred_element_type=jnp.float32)
    vocab_local = logits.shape[1]
    vocab_ids = my_rank * vocab_local + jnp.arange(vocab_local, dtype=jnp.int32)
    target_hit = vocab_ids[None, :] == targets[:, None]
    pick_local = jnp.sum(jnp.where(target_hit, logits, jnp.float32(0.0)), axis=-1)
    top_logit = lax.pmax(jnp.max(logits, axis=-1), "tensor")
    exp_local = jnp.sum(jnp.exp(logits - top_logit[:, None]), axis=-1)
    exp_total, target_logit = lax.psum((exp_local, pick_local), "tensor")
    log_total = top_logit + jnp.log(exp_total)
    logprob = logits - log_total[:, None]
    target_own = target_logit - log_total
    half_rows = row_count // 2
    keep_first = member_rank * half_rows
    send_first = (1 - member_rank) * half_rows
    keep_logprob = lax.dynamic_slice_in_dim(logprob, keep_first, half_rows, 0)
    keep_target = lax.dynamic_slice_in_dim(target_own, keep_first, half_rows, 0)
    send_logprob = lax.dynamic_slice_in_dim(logprob, send_first, half_rows, 0)
    send_target = lax.dynamic_slice_in_dim(target_own, send_first, half_rows, 0)
    other_logprob, other_target = swapped((send_logprob, send_target), "member", 0)
    return (0.5 * (keep_logprob + other_logprob), 0.5 * (keep_target + other_target))


def solution(mesh):
    placed = (
        P("member", "rep", None, None),
        P("member", "rep", "tensor", None),
        P("member", "rep", "tensor", None),
        P("rep"),
        P("rep"),
        P("member", "rep", None),
        P("member", "tensor", None),
        P("member", None),
        P("member", None, "tensor"),
    )
    return jax.shard_map(
        local,
        mesh=mesh,
        in_specs=placed,
        out_specs=(P(("rep", "member"), "tensor"), P(("rep", "member"))),
        check_vma=False,
    )
```

profile of v0, /device:TPU:1, one launch (start us, length us, event | category | flops | bytes accessed | tf_op | source)
XLA Modules:
  0.0 211.9 jit_solution(13294165735235029691)
XLA Ops:
  7.2 0.0 all-reduce.3.cloned.1.call-start
  7.3 0.9 broadcast_compare_fusion
  8.1 1.7 fusion.36
  9.8 0.2 fusion.7
  10.0 2.2 %collective-permute-start.4 = (bf16[8,8]{1,0:T(8,128)(2,1)S(1)}, bf16[8,8]{1,0:T(8,128)(2,1)S(1)}, u32[]{:S(2)}, u32[]{:S(2)}) collective-permute-start(bf16[8,8]{1,0:T(8,128)(2,1)S(1)} %convert_element_type.73), channel_id=1, source_target_pairs={{0,1},{1,0},{2,3},{3,2},{4,5},{5,4},{6,7},{7,6},{8,9},{9,8},{10,11... | collective-permute-start | bytes 392 | tf_op jit(solution)/shard_map/ppermute | solution.py:25
  12.2 0.1 collective-permute-start
  12.4 1.5 fusion.37
  13.9 1.4 collective-permute-start.1
  15.3 2.7 %collective-permute-start.5 = (bf16[8,8]{1,0:T(8,128)(2,1)S(1)}, bf16[8,8]{1,0:T(8,128)(2,1)S(1)}, u32[]{:S(2)}, u32[]{:S(2)}) collective-permute-start(bf16[8,8]{1,0:T(8,128)(2,1)S(1)} %get-tuple-element.13), channel_id=1, source_target_pairs={{0,2},{2,0},{1,3},{3,1},{4,6},{6,4},{5,7},{7,5},{8,10},{10,8},{9,1... | collective-permute-start | bytes 392 | tf_op jit(solution)/shard_map/ppermute | solution.py:25
  18.0 0.3 collective-permute-start.2
  18.4 1.0 collective-permute-done.5
  19.4 2.6 %collective-permute-done.2 = bf16[8,8]{1,0:T(8,128)(2,1)S(1)} collective-permute-done((bf16[8,8]{1,0:T(8,128)(2,1)S(1)}, bf16[8,8]{1,0:T(8,128)(2,1)S(1)}, u32[]{:S(2)}, u32[]{:S(2)}) %collective-permute-start.2) | collective-permute-done | bytes 160 | tf_op jit(solution)/shard_map/ppermute | solution.py:25
  22.0 0.1 constant_dynamic-slice_fusion
  22.1 0.1 fusion.31
  22.2 0.4 collective-permute-start.3
  22.6 0.1 constant_dynamic-slice_fusion.3
  22.7 3.7 %collective-permute-done.3 = bf16[8,8,128]{2,1,0:T(8,128)(2,1)S(1)} collective-permute-done((bf16[8,8,128]{2,1,0:T(8,128)(2,1)S(1)}, bf16[8,8,128]{2,1,0:T(8,128)(2,1)S(1)}, u32[]{:S(2)}, u32[]{:S(2)}) %collective-permute-start.3) | collective-permute-done | bytes 16416 | tf_op jit(solution)/shard_map/ppermute | solution.py:25
  26.4 0.1 fusion.26
  26.5 1.0 convolution_convert_fusion
  27.5 93.4 %all-reduce.3.cloned.1.call-done = bf16[8,4096]{1,0:T(8,128)(2,1)} async-done(((bf16[8,4096]{1,0:T(8,128)(2,1)}), bf16[8,4096]{1,0:T(8,128)(2,1)}) %all-reduce.3.cloned.1.call-update) | async-done | bytes 65552 | tf_op jit(solution)/shard_map/psum | solution.py:80
  120.9 1.0 multiply_reduce_fusion
  121.9 4.8 %fusion.38 = (f32[8]{0:T(128)S(1)}, f32[8,1024]{1,0:T(8,128)S(1)}) fusion(bf16[1,4096,1024]{2,1,0:T(8,128)(2,1)} %param.17, bf16[8,4096]{1,0:T(8,128)(2,1)} %all-reduce.3.cloned.1.call-done, bf16[1,8,4096]{2,1,0:T(8,128)(2,1)} %param.14, f32[4096]{0:T(1024)} %bitcast.38, f32[8]{0:T(128)S(1)} %add_rsqrt_fusion), kind=kOutput, calls=%fused_computation.63 | convolution fusion | flops 67313656 | bytes 8568896 | tf_op jit(solution)/shard_map/dot_general | solution.py:86
  126.8 30.9 %pmax.7 = f32[8]{0:T(128)S(1)} all-reduce(f32[8]{0:T(128)S(1)} %get-tuple-element.21), channel_id=1, replica_groups=mesh['member'=2,'rep'=8,'tensor'=16] {'tensor'}, use_global_device_ids=true, to_apply=%region_5.6 | all-reduce | flops 8 | bytes 64 | tf_op jit(solution)/shard_map/pmax | solution.py:91
  157.6 0.2 select_reduce_fusion
  157.9 28.5 %all-reduce = (f32[8]{0:T(128)S(1)}, f32[8]{0:T(128)S(1)}) all-reduce(f32[8]{0:T(128)S(1)} %get-tuple-element.3, f32[8]{0:T(128)S(1)} %get-tuple-element.2), channel_id=1, replica_groups=mesh['member'=2,'rep'=8,'tensor'=16] {'tensor'}, use_global_device_ids=true, to_apply=%region_7.8 | all-reduce | flops 16 | bytes 128 | tf_op jit(solution)/shard_map/psum | solution.py:93
  186.4 0.1 broadcast_subtract_fusion
  186.5 0.1 dynamic_slice.30
  186.5 16.5 %collective-permute-start.7 = (f32[4]{0:T(128)S(1)}, f32[4]{0:T(128)S(1)}, u32[]{:S(2)}, u32[]{:S(2)}) collective-permute-start(f32[4]{0:T(128)S(1)} %dynamic_slice.30), channel_id=1, source_target_pairs={{0,128},{128,0},{1,129},{129,1},{2,130},{130,2},{3,131},{131,3},{4... | collective-permute-start | bytes 56 | tf_op jit(solution)/shard_map/ppermute | solution.py:25
  203.0 0.1 collective-permute-start.6
  203.1 0.7 collective-permute-done.7
  203.8 0.6 add_multiply_fusion.1
  204.4 0.6 add_multiply_fusion
  (19 shorter events, 0.1 us)
Async XLA Ops:
  7.2 19.3 %copy-start = (bf16[1,256,4096]{2,1,0:T(8,128)(2,1)S(1)}, bf16[1,256,4096]{2,1,0:T(8,128)(2,1)}, u32[]{:S(2)}) copy-start(bf16[1,256,4096]{2,1,0:T(8,128)(2,1)} %param.15) | copy-start | bytes 6291460
  7.2 150.5 %copy-start.1 = (s32[8]{0:T(128)S(1)}, s32[8]{0:T(128)}, u32[]{:S(2)}) copy-start(s32[8]{0:T(128)} %param.13) | copy-start | bytes 100
  7.2 113.7 %all-reduce.3.cloned.1.call-start = ((), (), s32[]{:S(2)}) async-start(), calls=%async_computation | async-start | bytes 131072 | tf_op jit(solution)/shard_map/psum | solution.py:80
  10.0 5.3 %collective-permute-start.4 = (bf16[8,8]{1,0:T(8,128)(2,1)S(1)}, bf16[8,8]{1,0:T(8,128)(2,1)S(1)}, u32[]{:S(2)}, u32[]{:S(2)}) collective-permute-start(bf16[8,8]{1,0:T(8,128)(2,1)S(1)} %convert_element_type.73), channel_id=1, source_target_pairs={{0,1},{1,0},{2,3},{3,2},{4,5},{5,4},{6,7},{7,6},{8,9},{9,8},{10,11... | collective-permute-start | bytes 392 | tf_op jit(solution)/shard_map/ppermute | solution.py:25
  12.2 3.1 %collective-permute-start = (bf16[8,8]{1,0:T(8,128)(2,1)S(1)}, bf16[8,8]{1,0:T(8,128)(2,1)S(1)}, u32[]{:S(2)}, u32[]{:S(2)}) collective-permute-start(bf16[8,8]{1,0:T(8,128)(2,1)S(1)} %convert_element_type.65), channel_id=1, source_target_pairs={{0,1},{1,0},{2,3},{3,2},{4,5},{5,4},{6,7},{7,6},{8,9},{9,8},{10,11... | collective-permute-start | bytes 392 | tf_op jit(solution)/shard_map/ppermute | solution.py:25
  13.9 8.2 %collective-permute-start.1 = (bf16[8,8,128]{2,1,0:T(8,128)(2,1)S(1)}, bf16[8,8,128]{2,1,0:T(8,128)(2,1)S(1)}, u32[]{:S(2)}, u32[]{:S(2)}) collective-permute-start(bf16[8,8,128]{2,1,0:T(8,128)(2,1)S(1)} %get-tuple-element.19), channel_id=1, source_target_pairs={{0,1},{1,0},{2,3},{3,2},{4,5},{5,4},{6,7},{7,6},{8,9},{9,8},{10,11... | collective-permute-start | bytes 49160 | tf_op jit(solution)/shard_map/ppermute | solution.py:25
  15.3 4.0 %collective-permute-start.5 = (bf16[8,8]{1,0:T(8,128)(2,1)S(1)}, bf16[8,8]{1,0:T(8,128)(2,1)S(1)}, u32[]{:S(2)}, u32[]{:S(2)}) collective-permute-start(bf16[8,8]{1,0:T(8,128)(2,1)S(1)} %get-tuple-element.13), channel_id=1, source_target_pairs={{0,2},{2,0},{1,3},{3,1},{4,6},{6,4},{5,7},{7,5},{8,10},{10,8},{9,1... | collective-permute-start | bytes 392 | tf_op jit(solution)/shard_map/ppermute | solution.py:25
  18.0 3.9 %collective-permute-start.2 = (bf16[8,8]{1,0:T(8,128)(2,1)S(1)}, bf16[8,8]{1,0:T(8,128)(2,1)S(1)}, u32[]{:S(2)}, u32[]{:S(2)}) collective-permute-start(bf16[8,8]{1,0:T(8,128)(2,1)S(1)} %fusion.27), channel_id=1, source_target_pairs={{0,2},{2,0},{1,3},{3,1},{4,6},{6,4},{5,7},{7,5},{8,10},{10,8},{9,1... | collective-permute-start | bytes 392 | tf_op jit(solution)/shard_map/ppermute | solution.py:25
  22.2 4.2 %collective-permute-start.3 = (bf16[8,8,128]{2,1,0:T(8,128)(2,1)S(1)}, bf16[8,8,128]{2,1,0:T(8,128)(2,1)S(1)}, u32[]{:S(2)}, u32[]{:S(2)}) collective-permute-start(bf16[8,8,128]{2,1,0:T(8,128)(2,1)S(1)} %get-tuple-element.8), channel_id=1, source_target_pairs={{0,2},{2,0},{1,3},{3,1},{4,6},{6,4},{5,7},{7,5},{8,10},{10,8},{9,1... | collective-permute-start | bytes 49160 | tf_op jit(solution)/shard_map/ppermute | solution.py:25
  186.5 17.3 %collective-permute-start.7 = (f32[4]{0:T(128)S(1)}, f32[4]{0:T(128)S(1)}, u32[]{:S(2)}, u32[]{:S(2)}) collective-permute-start(f32[4]{0:T(128)S(1)} %dynamic_slice.30), channel_id=1, source_target_pairs={{0,128},{128,0},{1,129},{129,1},{2,130},{130,2},{3,131},{131,3},{4... | collective-permute-start | bytes 56 | tf_op jit(solution)/shard_map/ppermute | solution.py:25
  203.0 1.4 collective-permute-start.6
Sparse Core Ops, SparseCore 0:
  27.6 93.2 all-reduce.2
where the time goes:
time: 212 us
  waiting for transfers between devices  101 us (48%)
  blocking collectives  59.4 us (28%)
  starting transfers between devices  23.9 us (11%)
  between operations  14.1 us (7%)
  matrix products  9.04 us (4%)
  other arithmetic  3.79 us (2%)
    psum x1, waiting for transfers between devices, local(): lax.psum(projected.astype(jnp.bfloat16), 'tensor').astype(jnp.float32)  93.4 us
    pmax x1, blocking collectives, local(): top_logit = lax.pmax(jnp.max(logits, axis=-1), 'tensor')  30.9 us
    psum x1, blocking collectives, local(): exp_total, target_logit = lax.psum((exp_local, pick_local), 'tensor')  28.5 us
    ppermute x8, starting transfers between devices, swapped(): return lax.ppermute(block, axis, route)  23.8 us
    ppermute x8, waiting for transfers between devices, swapped(): return lax.ppermute(block, axis, route)  7.97 us
    dot_general x1, matrix products, local(): logits = jnp.dot(normed, head_weight[0], preferred_element_type=jnp.float32)  4.82 us
  transfers between devices with their start and end apart: 9, of which 5 were waited for; matrix products, arithmetic and copies ran while one was open for 1% of the time, Pallas kernels for 0%

commit v1 on v0

--- a/solution.py
+++ b/solution.py
@@ -77,7 +77,9 @@
     )
     projected = jnp.dot(attended, out_weight[0], preferred_element_type=jnp.float32)
     stream = residual[0].astype(jnp.float32)
-    summed = lax.psum(projected.astype(jnp.bfloat16), "tensor").astype(jnp.float32)
+    summed = jnp.sum(lax.all_gather(projected.astype(jnp.bfloat16), "tensor"), axis=0).astype(
+        jnp.float32
+    )
     hidden = stream + summed
     scaled = (
         hidden * lax.rsqrt(jnp.mean(hidden * hidden, axis=-1, keepdims=True) + 1e-05) * norm_gain[0]

time: 212 us -> 173 us (0.82)
  waiting for transfers between devices: 101 us -> 61.2 us
    psum x1 -> x0, waiting for transfers between devices: 93.4 us -> none  [local(): lax.psum(projected.astype(jnp.bfloat16), 'tensor').astype(jnp.float32)]
    all_gather x0 -> x1, waiting for transfers between devices: none -> 51.5 us  [local(): lax.all_gather(projected.astype(jnp.bfloat16), 'tensor')]
  transfers between devices with their start and end apart: 9 -> 9, of which waited for: 5 -> 6; matrix products, arithmetic and copies ran while one was open for 1% -> 1% of each run, Pallas kernels for 0% -> 0%
where the time goes in v1:
time: 173 us
  waiting for transfers between devices  61.2 us (35%)
  blocking collectives  59.9 us (35%)
  starting transfers between devices  22.8 us (13%)
  between operations  14.2 us (8%)
  matrix products  9.02 us (5%)
  other arithmetic  5.12 us (3%)
    all_gather x1, waiting for transfers between devices, local(): lax.all_gather(projected.astype(jnp.bfloat16), 'tensor')  51.5 us
    pmax x1, blocking collectives, local(): top_logit = lax.pmax(jnp.max(logits, axis=-1), 'tensor')  31.3 us
    psum x1, blocking collectives, local(): exp_total, target_logit = lax.psum((exp_local, pick_local), 'tensor')  28.6 us
    ppermute x8, starting transfers between devices, swapped(): return lax.ppermute(block, axis, route)  22.8 us
    ppermute x8, waiting for transfers between devices, swapped(): return lax.ppermute(block, axis, route)  9.64 us
    dot_general x1, matrix products, local(): logits = jnp.dot(normed, head_weight[0], preferred_element_type=jnp.float32)  4.78 us
  transfers between devices with their start and end apart: 9, of which 6 were waited for; matrix products, arithmetic and copies ran while one was open for 1% of the time, Pallas kernels for 0%

profile of v1, /device:TPU:1, one launch (start us, length us, event | category | flops | bytes accessed | tf_op | source)
XLA Modules:
  0.0 172.5 jit_solution(13018246748220882856)
XLA Ops:
  7.3 0.9 broadcast_compare_fusion
  8.1 1.7 fusion.42
  9.8 1.5 fusion.43
  11.4 2.2 %collective-permute-start.1 = (bf16[8,8,128]{2,1,0:T(8,128)(2,1)S(1)}, bf16[8,8,128]{2,1,0:T(8,128)(2,1)S(1)}, u32[]{:S(2)}, u32[]{:S(2)}) collective-permute-start(bf16[8,8,128]{2,1,0:T(8,128)(2,1)S(1)} %get-tuple-element.19), channel_id=1, source_target_pairs={{0,1},{1,0},{2,3},{3,2},{4,5},{5,4},{6,7},{7,6},{8,9},{9,8},{10,11... | collective-permute-start | bytes 49160 | tf_op jit(solution)/shard_map/ppermute | solution.py:25
  13.6 0.2 fusion.12
  13.8 0.1 collective-permute-start.4
  13.9 1.4 collective-permute-start
  15.3 1.1 collective-permute-done
  16.4 3.0 %collective-permute-start.2 = (bf16[8,8]{1,0:T(8,128)(2,1)S(1)}, bf16[8,8]{1,0:T(8,128)(2,1)S(1)}, u32[]{:S(2)}, u32[]{:S(2)}) collective-permute-start(bf16[8,8]{1,0:T(8,128)(2,1)S(1)} %fusion.33), channel_id=1, source_target_pairs={{0,2},{2,0},{1,3},{3,1},{4,6},{6,4},{5,7},{7,5},{8,10},{10,8},{9,1... | collective-permute-start | bytes 392 | tf_op jit(solution)/shard_map/ppermute | solution.py:25
  19.4 0.1 collective-permute-start.5
  19.5 0.9 collective-permute-done.2
  20.4 3.1 %collective-permute-done.5 = bf16[8,8]{1,0:T(8,128)(2,1)S(1)} collective-permute-done((bf16[8,8]{1,0:T(8,128)(2,1)S(1)}, bf16[8,8]{1,0:T(8,128)(2,1)S(1)}, u32[]{:S(2)}, u32[]{:S(2)}) %collective-permute-start.5) | collective-permute-done | bytes 160 | tf_op jit(solution)/shard_map/ppermute | solution.py:25
  23.4 0.1 constant_dynamic-slice_fusion
  23.5 0.1 fusion.37
  23.6 0.1 collective-permute-start.3
  23.7 0.1 constant_dynamic-slice_fusion.3
  23.8 4.0 %collective-permute-done.3 = bf16[8,8,128]{2,1,0:T(8,128)(2,1)S(1)} collective-permute-done((bf16[8,8,128]{2,1,0:T(8,128)(2,1)S(1)}, bf16[8,8,128]{2,1,0:T(8,128)(2,1)S(1)}, u32[]{:S(2)}, u32[]{:S(2)}) %collective-permute-start.3) | collective-permute-done | bytes 16416 | tf_op jit(solution)/shard_map/ppermute | solution.py:25
  27.8 0.1 fusion.32
  27.9 1.0 convolution_convert_fusion
  28.9 51.5 %all-gather.3.cloned.1.call-done = bf16[128,4096]{1,0:T(8,128)(2,1)} async-done(((bf16[8,4096]{1,0:T(8,128)(2,1)}), bf16[128,4096]{1,0:T(8,128)(2,1)}) %all-gather.3.cloned.1.call-update) | async-done | bytes 1048592 | tf_op jit(solution)/shard_map/all_gather | solution.py:80
  80.5 1.4 bitcast_reduce_fusion
  81.9 1.0 fusion.11
  82.9 4.8 %fusion.44 = (f32[8]{0:T(128)S(1)}, f32[8,1024]{1,0:T(8,128)S(1)}) fusion(bf16[1,4096,1024]{2,1,0:T(8,128)(2,1)} %param.17, bf16[8,4096]{1,0:T(8,128)(2,1)S(1)} %bitcast_reduce_fusion, bf16[1,8,4096]{2,1,0:T(8,128)(2,1)} %param.14, f32[4096]{0:T(1024)} %bitcast.53, f32[8]{0:T(128)S(1)} %add_rsqrt_fusion), kind=kOutput, calls=%fused_computation.70 | convolution fusion | flops 67313656 | bytes 8568896 | tf_op jit(solution)/shard_map/dot_general | solution.py:88
  87.6 31.3 %pmax.7 = f32[8]{0:T(128)S(1)} all-reduce(f32[8]{0:T(128)S(1)} %get-tuple-element.21), channel_id=1, replica_groups=mesh['member'=2,'rep'=8,'tensor'=16] {'tensor'}, use_global_device_ids=true, to_apply=%region_5.6 | all-reduce | flops 8 | bytes 64 | tf_op jit(solution)/shard_map/pmax | solution.py:93
  119.0 0.2 select_reduce_fusion
  119.2 28.6 %all-reduce = (f32[8]{0:T(128)S(1)}, f32[8]{0:T(128)S(1)}) all-reduce(f32[8]{0:T(128)S(1)} %get-tuple-element.3, f32[8]{0:T(128)S(1)} %get-tuple-element.2), channel_id=1, replica_groups=mesh['member'=2,'rep'=8,'tensor'=16] {'tensor'}, use_global_device_ids=true, to_apply=%region_7.8 | all-reduce | flops 16 | bytes 128 | tf_op jit(solution)/shard_map/psum | solution.py:95
  147.8 0.1 dynamic_slice.30
  147.9 15.8 %collective-permute-start.7 = (f32[4]{0:T(128)S(1)}, f32[4]{0:T(128)S(1)}, u32[]{:S(2)}, u32[]{:S(2)}) collective-permute-start(f32[4]{0:T(128)S(1)} %dynamic_slice.30), channel_id=1, source_target_pairs={{0,128},{128,0},{1,129},{129,1},{2,130},{130,2},{3,131},{131,3},{4... | collective-permute-start | bytes 56 | tf_op jit(solution)/shard_map/ppermute | solution.py:25
  163.7 0.1 collective-permute-start.6
  163.8 0.6 collective-permute-done.7
  164.5 0.6 add_multiply_fusion.1
  165.1 0.6 add_multiply_fusion
  (20 shorter events, 0.2 us)
Async XLA Ops:
  7.2 20.7 %copy-start = (bf16[1,256,4096]{2,1,0:T(8,128)(2,1)S(1)}, bf16[1,256,4096]{2,1,0:T(8,128)(2,1)}, u32[]{:S(2)}) copy-start(bf16[1,256,4096]{2,1,0:T(8,128)(2,1)} %param.15) | copy-start | bytes 6291460
  7.2 111.8 %copy-start.1 = (s32[8]{0:T(128)S(1)}, s32[8]{0:T(128)}, u32[]{:S(2)}) copy-start(s32[8]{0:T(128)} %param.13) | copy-start | bytes 100
  7.2 73.3 %all-gather.3.cloned.1.call-start = ((), (), s32[]{:S(2)}) async-start(), calls=%async_computation | async-start | bytes 1114112 | tf_op jit(solution)/shard_map/all_gather | solution.py:80
  11.4 12.1 %collective-permute-start.1 = (bf16[8,8,128]{2,1,0:T(8,128)(2,1)S(1)}, bf16[8,8,128]{2,1,0:T(8,128)(2,1)S(1)}, u32[]{:S(2)}, u32[]{:S(2)}) collective-permute-start(bf16[8,8,128]{2,1,0:T(8,128)(2,1)S(1)} %get-tuple-element.19), channel_id=1, source_target_pairs={{0,1},{1,0},{2,3},{3,2},{4,5},{5,4},{6,7},{7,6},{8,9},{9,8},{10,11... | collective-permute-start | bytes 49160 | tf_op jit(solution)/shard_map/ppermute | solution.py:25
  13.8 5.6 %collective-permute-start.4 = (bf16[8,8]{1,0:T(8,128)(2,1)S(1)}, bf16[8,8]{1,0:T(8,128)(2,1)S(1)}, u32[]{:S(2)}, u32[]{:S(2)}) collective-permute-start(bf16[8,8]{1,0:T(8,128)(2,1)S(1)} %convert_element_type.92), channel_id=1, source_target_pairs={{0,1},{1,0},{2,3},{3,2},{4,5},{5,4},{6,7},{7,6},{8,9},{9,8},{10,11... | collective-permute-start | bytes 392 | tf_op jit(solution)/shard_map/ppermute | solution.py:25
  13.9 2.5 %collective-permute-start = (bf16[8,8]{1,0:T(8,128)(2,1)S(1)}, bf16[8,8]{1,0:T(8,128)(2,1)S(1)}, u32[]{:S(2)}, u32[]{:S(2)}) collective-permute-start(bf16[8,8]{1,0:T(8,128)(2,1)S(1)} %convert_element_type.84), channel_id=1, source_target_pairs={{0,1},{1,0},{2,3},{3,2},{4,5},{5,4},{6,7},{7,6},{8,9},{9,8},{10,11... | collective-permute-start | bytes 392 | tf_op jit(solution)/shard_map/ppermute | solution.py:25
  16.4 3.9 %collective-permute-start.2 = (bf16[8,8]{1,0:T(8,128)(2,1)S(1)}, bf16[8,8]{1,0:T(8,128)(2,1)S(1)}, u32[]{:S(2)}, u32[]{:S(2)}) collective-permute-start(bf16[8,8]{1,0:T(8,128)(2,1)S(1)} %fusion.33), channel_id=1, source_target_pairs={{0,2},{2,0},{1,3},{3,1},{4,6},{6,4},{5,7},{7,5},{8,10},{10,8},{9,1... | collective-permute-start | bytes 392 | tf_op jit(solution)/shard_map/ppermute | solution.py:25
  19.4 4.0 %collective-permute-start.5 = (bf16[8,8]{1,0:T(8,128)(2,1)S(1)}, bf16[8,8]{1,0:T(8,128)(2,1)S(1)}, u32[]{:S(2)}, u32[]{:S(2)}) collective-permute-start(bf16[8,8]{1,0:T(8,128)(2,1)S(1)} %get-tuple-element.13), channel_id=1, source_target_pairs={{0,2},{2,0},{1,3},{3,1},{4,6},{6,4},{5,7},{7,5},{8,10},{10,8},{9,1... | collective-permute-start | bytes 392 | tf_op jit(solution)/shard_map/ppermute | solution.py:25
  23.6 4.2 %collective-permute-start.3 = (bf16[8,8,128]{2,1,0:T(8,128)(2,1)S(1)}, bf16[8,8,128]{2,1,0:T(8,128)(2,1)S(1)}, u32[]{:S(2)}, u32[]{:S(2)}) collective-permute-start(bf16[8,8,128]{2,1,0:T(8,128)(2,1)S(1)} %get-tuple-element.8), channel_id=1, source_target_pairs={{0,2},{2,0},{1,3},{3,1},{4,6},{6,4},{5,7},{7,5},{8,10},{10,8},{9,1... | collective-permute-start | bytes 49160 | tf_op jit(solution)/shard_map/ppermute | solution.py:25
  147.9 16.6 %collective-permute-start.7 = (f32[4]{0:T(128)S(1)}, f32[4]{0:T(128)S(1)}, u32[]{:S(2)}, u32[]{:S(2)}) collective-permute-start(f32[4]{0:T(128)S(1)} %dynamic_slice.30), channel_id=1, source_target_pairs={{0,128},{128,0},{1,129},{129,1},{2,130},{130,2},{3,131},{131,3},{4... | collective-permute-start | bytes 56 | tf_op jit(solution)/shard_map/ppermute | solution.py:25
  163.7 1.3 collective-permute-start.6
Sparse Core Ops, SparseCore 0:
  29.0 51.4 all-gather.2
